TPU v7x, 128 devices: a whole 4x4x4 slice. The times are simulated.
128 devices in a mesh: pipe: 32 (over y, z, x_hi), expert: 4 (over x_lo, core).
Axes of the slice: x: 4 (x_hi: 2, x_lo: 2; x = x_hi * 2 + x_lo), y: 4, z: 4, core: 2. Of those that a mesh axis runs over, the one named last changes fastest.
Arguments:
- fwd_in: bfloat16 [16384, 3584], P(('pipe', 'expert')), may hold values from -6 to 6
- fwd_routes: int32 [16384, 2], P(('pipe', 'expert')), may hold values from 0 to 3, all different within a row; in each aligned block of 128 rows (0 to 127, 128 to 255, ...) at most 96 rows name the same one
- saved_in: bfloat16 [16384, 3584], P(('pipe', 'expert')), may hold values from -6 to 6
- saved_routes: int32 [16384, 2], P(('pipe', 'expert')), may hold values from 0 to 3, all different within a row; in each aligned block of 128 rows (0 to 127, 128 to 255, ...) at most 96 rows name the same one
- grad_in: bfloat16 [16384, 3584], P(('pipe', 'expert')), may hold values from -6 to 6
- norm_gain: float32 [32, 3584], P('pipe'), may hold values from 0.25 to 1.75
- router: bfloat16 [32, 3584, 4], P('pipe'), may hold values from -0.09375 to 0.09375
- w_gate: bfloat16 [32, 4, 3584, 1024], P('pipe', 'expert'), may hold values from -0.09375 to 0.09375
- w_up: bfloat16 [32, 4, 3584, 1024], P('pipe', 'expert'), may hold values from -0.09375 to 0.09375
- w_down: bfloat16 [32, 4, 1024, 3584], P('pipe', 'expert'), may hold values from -0.1875 to 0.1875
Outputs:
- fwd_out: bfloat16 [16384, 3584], P(('pipe', 'expert'))
- grad_out: bfloat16 [16384, 3584], P(('pipe', 'expert'))
Inputs may be any that keep to these rules, and one draw needn't show every extreme that they name: `fwd_routes`: each row names 2 different experts; among the rows of one device no expert is named by more than 96 rows, a bound that some block reaches. `saved_routes`: each row names 2 different experts; among the rows of one device no expert is named by more than 96 rows, a bound that some block reaches.
All inputs are finite; a program needn't handle non-finite values.
Results may differ from a plain program's by a relative error of at most 0.0057.
Values may be sent and summed in bfloat16 or wider, within the bound.
A program may use at most 128 MiB of HBM per device.

v0:
```python
import functools

import jax
import jax.numpy as jnp
from jax import lax
from jax.experimental import pallas as pl
from jax.experimental.pallas import tpu as pltpu
from jax.sharding import PartitionSpec as P

EPSILON = 1e-06
MESH = pl.DeviceIdType.MESH
F32 = jnp.float32
BF16 = jnp.bfloat16
NT = (((1,), (1,)), ((), ()))
CHUNK = 32
STEP = 16


def kernel(
    n_pipe, tn, td,
    sx_hbm, z_hbm, fx_hbm, rt_in, gain, rout, wg_hbm, wu_hbm, wd_hbm,
    fo_hbm, go_hbm,
    sx, z, fx, rts, wg, wu, wd, rb, nrm, hh, dg, du, acc, cols, wb, wf, rcb, rcf, lpb, lpf, at, ar,
    loc_sem, w_sem, c_send, c_recv, l_send, l_recv, t_send, t_recv, pb_send, pb_recv, pf_send, pf_recv,
    go_send, go_recv, fo_send, fo_recv, zero_sem,
):
    c = lax.axis_index("pipe")
    e = lax.axis_index("expert")
    rows, width = sx_hbm.shape
    hidden = hh.shape[1]
    e_c = e + 1 - 2 * lax.rem(e, 2)
    e_l = lax.rem(e + 2, 4)
    e_d = lax.rem(e_c + 2, 4)
    core, link, diag = (c, e_c), (c, e_l), (c, e_d)
    after, before = (c + 1, e_l), (c - 1, e_l)
    n_chunks = rows // CHUNK

    def block(s):
        return pl.ds(s * rows, rows)

    def remote(src, dst, send, recv, to):
        return pltpu.make_async_remote_copy(
            src_ref=src, dst_ref=dst, send_sem=send, recv_sem=recv, device_id=to, device_id_type=MESH
        )

    def load_x(i):
        src, dst = ((sx_hbm, sx), (z_hbm, z), (fx_hbm, fx))[i]
        return pltpu.make_async_copy(src, dst.at[block(0)], loc_sem.at[i])

    def load_w(i, j):
        part = pl.ds(pl.multiple_of(j * tn, tn), tn)
        if i == 2:
            return pltpu.make_async_copy(wd_hbm.at[0, 0, part], wd.at[part], w_sem.at[i, j])
        src, dst = ((wg_hbm, wg), (wu_hbm, wu))[i]
        return pltpu.make_async_copy(src.at[0, 0, :, part], dst.at[:, part], w_sem.at[i, j])

    def own_to_core(i):
        src, dst = ((sx_hbm, sx), (z_hbm, z), (fx_hbm, fx))[i]
        return remote(src, dst.at[block(1)], c_send.at[i], c_recv.at[i], core)

    def own_to_link(i):
        src, dst = ((sx_hbm, sx), (z_hbm, z), (fx_hbm, fx))[i]
        return remote(src, dst.at[block(2)], l_send.at[i], l_recv.at[i], link)

    def pass_to_core(i):
        ref = (sx, z, fx)[i]
        return remote(ref.at[block(2)], ref.at[block(3)], c_send.at[3 + i], c_recv.at[3 + i], core)

    def sums_to_core(i, g):
        src, dst = ((wb, rcb), (wf, rcf))[i]
        k = 6 + 2 * i + g
        return remote(src.at[block(2 * g + 1)], dst.at[block(g)], c_send.at[k], c_recv.at[k], core)

    def routes_to(s):
        return remote(rt_in, rts.at[s], t_send.at[s - 1], t_recv.at[s - 1], (core, link, diag)[s - 1])

    def dots_to(s):
        t = (None, 3, 0, 1)[s]
        return remote(at.at[t], ar.at[s], t_send.at[2 + s], t_recv.at[2 + s], (core, link, diag)[s - 1])

    def part(q):
        return pl.ds(pl.multiple_of(q * CHUNK, CHUNK), CHUNK)

    def tail(q):
        return pl.ds(pl.multiple_of(2 * rows + q * CHUNK, CHUNK), CHUNK)

    def sums_to_link(i, q):
        src, dst, send, recv = ((wb, lpb, pb_send, pb_recv), (wf, lpf, pf_send, pf_recv))[i]
        return remote(src.at[part(q)], dst.at[part(q)], send.at[q], recv.at[q], link)

    def result(i, q):
        if i == 0:
            return remote(wb.at[tail(q)], go_hbm.at[part(q)], go_send.at[q], go_recv.at[q], before)
        return remote(wf.at[tail(q)], fo_hbm.at[part(q)], fo_send.at[q], fo_recv.at[q], after)

    tiles = hidden // tn
    load_x(0).start()
    for j in range(tiles):
        load_w(0, j).start()
        load_w(1, j).start()
        if j == 0:
            load_x(1).start()
        load_w(2, j).start()
    load_x(2).start()

    barrier = pltpu.get_barrier_semaphore()
    ring = [(lax.rem(c + by, n_pipe), e_l) for by in (1, n_pipe - 1)]
    for peer in (core, link, diag, *ring):
        pl.semaphore_signal(barrier, inc=1, device_id=peer, device_id_type=MESH)
    pl.semaphore_wait(barrier, 5)

    for s in (1, 2, 3):
        routes_to(s).start()
    for i in range(3):
        own_to_link(i).start()
        own_to_core(i).start()

    rts[0] = rt_in[...]
    rb[...] = jnp.zeros_like(rb)
    rb[0:16, :] = rout[...]
    eye = lax.broadcasted_iota(jnp.int32, (rows, rows), 0) == lax.broadcasted_iota(jnp.int32, (rows, rows), 1)

    def to_col(row):
        return jnp.sum(jnp.where(eye, row, 0.0), axis=1, keepdims=True)

    def to_row(col):
        return jnp.sum(jnp.where(eye, col, 0.0), axis=0, keepdims=True)

    def normalize(x_ref, g):
        def step(q, _):
            at_rows = pl.ds(pl.multiple_of(2 * g * rows + q * STEP, STEP), STEP)
            to_rows = pl.ds(pl.multiple_of(q * STEP, STEP), STEP)
            wide = x_ref[at_rows, :].astype(F32)
            inv = lax.rsqrt(jnp.mean(wide * wide, axis=1, keepdims=True) + EPSILON)
            nrm[to_rows, :] = (wide * inv * gain[...]).astype(BF16)
            return 0

        lax.fori_loop(0, 2 * rows // STEP, step, 0)

    def route_weights(g, kind):
        logits = lax.dot_general(nrm[...], rb[...], NT, preferred_element_type=F32)
        scores = jax.nn.sigmoid(logits)
        lane = lax.broadcasted_iota(jnp.int32, (rows, 128), 1).astype(F32)
        me = e.astype(F32)
        out = []
        for h in range(2):
            s = 2 * g + h
            tile = rts[s]
            first = 2 - 2 * kind
            r0, r1 = to_col(tile[first : first + 1, :]), to_col(tile[first + 1 : first + 2, :])
            mine = scores[h * rows : (h + 1) * rows, :]
            q0 = jnp.sum(jnp.where(lane == r0, mine, 0.0), axis=1, keepdims=True)
            q1 = jnp.sum(jnp.where(lane == r1, mine, 0.0), axis=1, keepdims=True)
            total = q0 + q1
            out.append(jnp.where(r0 == me, q0 / total, 0.0) + jnp.where(r1 == me, q1 / total, 0.0))
            if s == 2 and kind == 0:
                cols[...] = jnp.where(lane == 0.0, q0, jnp.where(lane == 1.0, q1, 0.0))
        return jnp.concatenate(out, axis=0)

    def backward(g, first):
        normalize(sx, g)
        weight = route_weights(g, 0)
        here = pl.ds(2 * g * rows, 2 * rows)

        def hidden_step(j, _):
            cut = pl.ds(pl.multiple_of(j * tn, tn), tn)
            if first:
                for i in range(3):
                    load_w(i, j).wait()
            gate = jnp.dot(nrm[...], wg[:, cut], preferred_element_type=F32)
            up = jnp.dot(nrm[...], wu[:, cut], preferred_element_type=F32)
            dhid = lax.dot_general(z[here, :], wd[cut, :], NT, preferred_element_type=F32)
            sig = jax.nn.sigmoid(gate)
            silu = gate * sig
            hh[:, cut] = (silu * up).astype(BF16)
            dg[:, cut] = (dhid * up * sig * (1.0 + gate * (1.0 - sig))).astype(BF16)
            du[:, cut] = (dhid * silu).astype(BF16)
            return 0

        lax.fori_loop(0, tiles, hidden_step, 0)
        acc[...] = jnp.zeros_like(acc)

        def model_step(j, _):
            cut = pl.ds(pl.multiple_of(j * td, td), td)
            out = jnp.dot(hh[...], wd[:, cut], preferred_element_type=F32).astype(BF16).astype(F32)
            prod = z[here, cut].astype(F32) * out
            folded = prod[:, 0:128]
            for k in range(1, td // 128):
                folded = folded + prod[:, k * 128 : (k + 1) * 128]
            acc[...] += folded
            dn = lax.dot_general(dg[...], wg[cut, :], NT, preferred_element_type=F32)
            dn = dn + lax.dot_general(du[...], wu[cut, :], NT, preferred_element_type=F32)
            wb[here, cut] = (weight * dn.astype(BF16).astype(F32)).astype(BF16)
            return 0

        lax.fori_loop(0, width // td, model_step, 0)
        dots = jnp.sum(acc[...], axis=1, keepdims=True).astype(BF16).astype(F32)
        for h in range(2):
            row = to_row(dots[h * rows : (h + 1) * rows, :])
            at[2 * g + h] = jnp.broadcast_to(row, (8, rows))

    def forward(g):
        normalize(fx, g)
        weight = route_weights(g, 1)
        here = pl.ds(2 * g * rows, 2 * rows)

        def hidden_step(j, _):
            cut = pl.ds(pl.multiple_of(j * tn, tn), tn)
            gate = jnp.dot(nrm[...], wg[:, cut], preferred_element_type=F32)
            up = jnp.dot(nrm[...], wu[:, cut], preferred_element_type=F32)
            hh[:, cut] = (gate * jax.nn.sigmoid(gate) * up).astype(BF16)
            return 0

        lax.fori_loop(0, tiles, hidden_step, 0)

        def model_step(j, _):
            cut = pl.ds(pl.multiple_of(j * td, td), td)
            out = jnp.dot(hh[...], wd[:, cut], preferred_element_type=F32).astype(BF16).astype(F32)
            wf[here, cut] = (weight * out).astype(BF16)
            return 0

        lax.fori_loop(0, width // td, model_step, 0)

    def chip_sums(i):
        keep, got = ((wb, rcb), (wf, rcf))[i]
        sums_to_core(i, 0).wait_recv()

        def step(q, _):
            keep[part(q), :] = (keep[part(q), :].astype(F32) + got[part(q), :].astype(F32)).astype(BF16)
            sums_to_link(i, q).start()
            return 0

        lax.fori_loop(0, n_chunks, step, 0)

    load_x(0).wait()
    load_x(1).wait()
    own_to_core(0).wait_recv()
    own_to_core(1).wait_recv()
    for s in (1, 2, 3):
        routes_to(s).wait_recv()
    backward(0, True)
    sums_to_core(0, 0).start()
    dots_to(2).start()
    dots_to(3).start()
    load_x(2).wait()
    own_to_core(2).wait_recv()
    own_to_link(0).wait_recv()
    pass_to_core(0).start()
    forward(0)
    sums_to_core(1, 0).start()
    chip_sums(0)
    own_to_link(1).wait_recv()
    pass_to_core(1).start()
    chip_sums(1)

    pass_to_core(0).wait_recv()
    pass_to_core(1).wait_recv()
    backward(1, False)
    sums_to_core(0, 1).start()
    dots_to(1).start()
    own_to_link(2).wait_recv()
    pass_to_core(2).start()
    pass_to_core(2).wait_recv()
    forward(1)
    sums_to_core(1, 1).start()
    nrm[0:rows, :] = jnp.zeros((rows, width), BF16)

    @pl.when(c == 0)
    def _():
        pltpu.make_async_copy(nrm.at[0:rows], fo_hbm, zero_sem.at[0]).start()

    @pl.when(c == n_pipe - 1)
    def _():
        pltpu.make_async_copy(nrm.at[0:rows], go_hbm, zero_sem.at[1]).start()

    for s in (1, 2, 3):
        dots_to(s).wait_recv()
    tile = rts[2]
    r0, r1 = to_col(tile[2:3, :]), to_col(tile[3:4, :])
    saved = cols[...]
    q0, q1 = saved[:, 0:1], saved[:, 1:2]
    total = q0 + q1
    a0, a1 = jnp.zeros((rows, 1), F32), jnp.zeros((rows, 1), F32)
    for s, owner in enumerate((e, e_c, e_l, e_d)):
        got = at[2] if s == 0 else ar[s]
        dot_col = to_col(got[0:1, :])
        a0 = a0 + jnp.where(r0 == owner.astype(F32), dot_col, 0.0)
        a1 = a1 + jnp.where(r1 == owner.astype(F32), dot_col, 0.0)
    mixed = a0 * (q0 / total) + a1 * (q1 / total)
    l0 = (a0 - mixed) / total * q0 * (1.0 - q0)
    l1 = (a1 - mixed) / total * q1 * (1.0 - q1)
    lane = lax.broadcasted_iota(jnp.int32, (rows, 128), 1).astype(F32)
    cols[...] = jnp.where(lane == r0, l0, 0.0) + jnp.where(lane == r1, l1, 0.0)
    sums_to_core(0, 1).wait_recv()

    def finish_backward(q, _):
        sums_to_link(0, q).wait_recv()
        for k in range(CHUNK // STEP):
            at_rows = pl.ds(pl.multiple_of(q * CHUNK + k * STEP, STEP), STEP)
            far = pl.ds(pl.multiple_of(2 * rows + q * CHUNK + k * STEP, STEP), STEP)
            near = pl.ds(pl.multiple_of(rows + q * CHUNK + k * STEP, STEP), STEP)
            wide = sx[far, :].astype(F32)
            inv = lax.rsqrt(jnp.mean(wide * wide, axis=1, keepdims=True) + EPSILON)
            dn = wb[far, :].astype(F32) + rcb[near, :].astype(F32) + lpb[at_rows, :].astype(F32)
            lcol = cols[at_rows, :]
            for j in range(4):
                dn = dn + lcol[:, j : j + 1] * rout[j : j + 1, :].astype(F32)
            scaled = dn * gain[...]
            mean = jnp.mean(scaled * wide, axis=1, keepdims=True)
            grad = z[far, :].astype(F32) + (inv * scaled - wide * (inv * inv * inv * mean))
            wb[far, :] = grad.astype(BF16)

        @pl.when(c > 0)
        def _():
            result(0, q).start()

        return 0

    lax.fori_loop(0, n_chunks, finish_backward, 0)
    sums_to_core(1, 1).wait_recv()

    def finish_forward(q, _):
        sums_to_link(1, q).wait_recv()
        for k in range(CHUNK // STEP):
            at_rows = pl.ds(pl.multiple_of(q * CHUNK + k * STEP, STEP), STEP)
            far = pl.ds(pl.multiple_of(2 * rows + q * CHUNK + k * STEP, STEP), STEP)
            near = pl.ds(pl.multiple_of(rows + q * CHUNK + k * STEP, STEP), STEP)
            out = wf[far, :].astype(F32) + rcf[near, :].astype(F32) + lpf[at_rows, :].astype(F32)
            wf[far, :] = (fx[far, :].astype(F32) + out).astype(BF16)

        @pl.when(c < n_pipe - 1)
        def _():
            result(1, q).start()

        return 0

    lax.fori_loop(0, n_chunks, finish_forward, 0)

    for s in (1, 2, 3):
        routes_to(s).wait_send()
        dots_to(s).wait_send()
    for i in range(3):
        own_to_core(i).wait_send()
        own_to_link(i).wait_send()
        pass_to_core(i).wait_send()
    for i in range(2):
        for g in range(2):
            sums_to_core(i, g).wait_send()
        for q in range(n_chunks):
            sums_to_link(i, q).wait_send()

    @pl.when(c > 0)
    def _():
        for q in range(n_chunks):
            result(0, q).wait_send()
            result(1, q).wait_recv()

    @pl.when(c < n_pipe - 1)
    def _():
        for q in range(n_chunks):
            result(1, q).wait_send()
            result(0, q).wait_recv()

    @pl.when(c == 0)
    def _():
        pltpu.make_async_copy(nrm.at[0:rows], fo_hbm, zero_sem.at[0]).wait()

    @pl.when(c == n_pipe - 1)
    def _():
        pltpu.make_async_copy(nrm.at[0:rows], go_hbm, zero_sem.at[1]).wait()


def local(
    n_pipe, fwd_in, fwd_routes, saved_in, saved_routes, grad_in, norm_gain, router, w_gate, w_up, w_down
):
    rows, width = fwd_in.shape
    hidden = w_gate.shape[3]
    tn = min(256, hidden)
    td = 512 if width % 512 == 0 else 128
    routes = jnp.concatenate([fwd_routes.T, saved_routes.T, fwd_routes.T, saved_routes.T], axis=0).astype(F32)
    rout = jnp.pad(router[0].T, ((0, 12), (0, 0)))
    n_chunks = rows // CHUNK
    dma = pltpu.SemaphoreType.DMA
    vmem = pl.BlockSpec(memory_space=pltpu.VMEM)
    hbm = pl.BlockSpec(memory_space=pl.ANY)
    grad_out_type = jax.ShapeDtypeStruct((rows, width), BF16)
    fwd_out, grad_out = pl.pallas_call(
        functools.partial(kernel, n_pipe, tn, td),
        out_shape=(grad_out_type, grad_out_type),
        in_specs=[hbm, hbm, hbm, vmem, vmem, vmem, hbm, hbm, hbm],
        out_specs=(hbm, hbm),
        scratch_shapes=[
            pltpu.VMEM((4 * rows, width), BF16),
            pltpu.VMEM((4 * rows, width), BF16),
            pltpu.VMEM((4 * rows, width), BF16),
            pltpu.VMEM((4, 8, rows), F32),
            pltpu.VMEM((width, hidden), BF16),
            pltpu.VMEM((width, hidden), BF16),
            pltpu.VMEM((hidden, width), BF16),
            pltpu.VMEM((128, width), BF16),
            pltpu.VMEM((2 * rows, width), BF16),
            pltpu.VMEM((2 * rows, hidden), BF16),
            pltpu.VMEM((2 * rows, hidden), BF16),
            pltpu.VMEM((2 * rows, hidden), BF16),
            pltpu.VMEM((2 * rows, 128), F32),
            pltpu.VMEM((rows, 128), F32),
            pltpu.VMEM((4 * rows, width), BF16),
            pltpu.VMEM((4 * rows, width), BF16),
            pltpu.VMEM((2 * rows, width), BF16),
            pltpu.VMEM((2 * rows, width), BF16),
            pltpu.VMEM((rows, width), BF16),
            pltpu.VMEM((rows, width), BF16),
            pltpu.VMEM((4, 8, rows), F32),
            pltpu.VMEM((4, 8, rows), F32),
            dma((3,)), dma((3, hidden // tn)),
            dma((10,)), dma((10,)),
            dma((3,)), dma((3,)),
            dma((6,)), dma((6,)),
            dma((n_chunks,)), dma((n_chunks,)),
            dma((n_chunks,)), dma((n_chunks,)),
            dma((n_chunks,)), dma((n_chunks,)),
            dma((n_chunks,)), dma((n_chunks,)),
            dma((2,)),
        ],
        compiler_params=pltpu.CompilerParams(
            collective_id=0, has_side_effects=True, vmem_limit_bytes=67043328
        ),
        name="relay_slot",
    )(saved_in, grad_in, fwd_in, routes, norm_gain, rout, w_gate, w_up, w_down)
    return fwd_out, grad_out


def solution(mesh):
    rows = P(("pipe", "expert"), None)
    in_specs = (
        rows, rows, rows, rows, rows,
        P("pipe", None),
        P("pipe", None, None),
        P("pipe", "expert", None, None),
        P("pipe", "expert", None, None),
        P("pipe", "expert", None, None),
    )
    return jax.shard_map(
        functools.partial(local, mesh.shape["pipe"]),
        mesh=mesh, in_specs=in_specs, out_specs=(rows, rows), check_vma=False,
    )
```

profile of v0, /device:TPU:24, one launch (start us, length us, event | category | flops | bytes accessed | tf_op | source)
XLA Modules:
  0.0 133.0 jit_solution(9498152982901443044)
XLA Ops:
  0.6 1.4 %add_convert_fusion.rt_in = f32[8,128]{1,0:T(8,128)} fusion(s32[2,128]{1,0:T(2,128)} %bitcast.6, s32[2,128]{1,0:T(2,128)} %bitcast.7), kind=kLoop, calls=%fused_computation | loop fusion | flops 4096 | bytes 6144 | tf_op jit(solution)/shard_map/convert_element_type | solution.py:380
  2.0 1.4 %pad.4.rout = bf16[16,3584]{1,0:T(8,128)(2,1)} pad(bf16[4,3584]{1,0:T(4,128)(2,1)} %bitcast.5, bf16[]{:T(256)} %constant.2.clone.1), padding=0_12x0_0 | pad | bytes 143362 | tf_op jit(solution)/shard_map/jit(_pad)/pad | solution.py:381
  3.4 125.3 %relay_slot.1 = (bf16[128,3584]{1,0:T(8,128)(2,1)}, bf16[128,3584]{1,0:T(8,128)(2,1)}) custom-call(bf16[128,3584]{1,0:T(8,128)(2,1)} %sx_hbm.1, bf16[128,3584]{1,0:T(8,128)(2,1)} %z_hbm.1, bf16[128,3584]{1,0:T(8,128)(2,1)} %fx_hbm.1, f32[8,128]{1,0:T(8,128)} %add_convert_fusion.rt_in, f32[1,3584]{1,0:T(1,128)} %gain.1, bf16[16,3584]{1,0:T(8,128)(2,1)} %pad.4.rout, ...), custom_call_target="tpu_custom_call" | custom-call | tf_op jit(solution)/shard_map/relay_slot/pallas_call | solution.py:387
  128.7 2.2 %copy.14 = bf16[128,3584]{1,0:T(8,128)(2,1)} copy(bf16[128,3584]{1,0:T(8,128)(2,1)} %get-tuple-element.4) | data formatting | bytes 1835008
  130.9 2.2 %copy.15 = bf16[128,3584]{1,0:T(8,128)(2,1)} copy(bf16[128,3584]{1,0:T(8,128)(2,1)} %get-tuple-element.5) | data formatting | bytes 1835008
where the time goes:
time: 133 us
  Pallas kernels  125 us (94%)
  local copies, waits for them, and re-layouts  5.73 us (4%)
  other arithmetic  1.36 us (1%)
    pallas_call x1, Pallas kernels, local(): pl.pallas_call(functools.partial(kernel, n_pipe, tn, td), out_shape=(grad...  125 us
    unnamed x2, local copies, waits for them, and re-layouts  4.32 us

commit v1 on v0

--- a/solution.py
+++ b/solution.py
@@ -12,7 +12,7 @@
 F32 = jnp.float32
 BF16 = jnp.bfloat16
 NT = (((1,), (1,)), ((), ()))
-CHUNK = 32
+CHUNK = 16
 STEP = 16
 
 
@@ -199,7 +199,7 @@
             row = to_row(dots[h * rows : (h + 1) * rows, :])
             at[2 * g + h] = jnp.broadcast_to(row, (8, rows))
 
-    def forward(g):
+    def forward(g, between=None):
         normalize(fx, g)
         weight = route_weights(g, 1)
         here = pl.ds(2 * g * rows, 2 * rows)
@@ -209,6 +209,8 @@
             gate = jnp.dot(nrm[...], wg[:, cut], preferred_element_type=F32)
             up = jnp.dot(nrm[...], wu[:, cut], preferred_element_type=F32)
             hh[:, cut] = (gate * jax.nn.sigmoid(gate) * up).astype(BF16)
+            if between is not None:
+                between(j)
             return 0
 
         lax.fori_loop(0, tiles, hidden_step, 0)
@@ -260,19 +262,6 @@
     dots_to(1).start()
     own_to_link(2).wait_recv()
     pass_to_core(2).start()
-    pass_to_core(2).wait_recv()
-    forward(1)
-    sums_to_core(1, 1).start()
-    nrm[0:rows, :] = jnp.zeros((rows, width), BF16)
-
-    @pl.when(c == 0)
-    def _():
-        pltpu.make_async_copy(nrm.at[0:rows], fo_hbm, zero_sem.at[0]).start()
-
-    @pl.when(c == n_pipe - 1)
-    def _():
-        pltpu.make_async_copy(nrm.at[0:rows], go_hbm, zero_sem.at[1]).start()
-
     for s in (1, 2, 3):
         dots_to(s).wait_recv()
     tile = rts[2]
@@ -316,7 +305,22 @@
 
         return 0
 
-    lax.fori_loop(0, n_chunks, finish_backward, 0)
+    early = n_chunks - tiles - 2
+    lax.fori_loop(0, early, finish_backward, 0)
+    pass_to_core(2).wait_recv()
+    forward(1, lambda j: finish_backward(early + j, 0))
+    sums_to_core(1, 1).start()
+    lax.fori_loop(early + tiles, n_chunks, finish_backward, 0)
+    nrm[0:rows, :] = jnp.zeros((rows, width), BF16)
+
+    @pl.when(c == 0)
+    def _():
+        pltpu.make_async_copy(nrm.at[0:rows], fo_hbm, zero_sem.at[0]).start()
+
+    @pl.when(c == n_pipe - 1)
+    def _():
+        pltpu.make_async_copy(nrm.at[0:rows], go_hbm, zero_sem.at[1]).start()
+
     sums_to_core(1, 1).wait_recv()
 
     def finish_forward(q, _):

time: 133 us -> 124 us (0.932)
  Pallas kernels: 125 us -> 116 us
    pallas_call x1, Pallas kernels: 125 us -> 116 us  [local(): pl.pallas_call(functools.partial(kernel, n_pipe, tn, td), out_shape=(grad...]
where the time goes in v1:
time: 124 us; the launch traced here: 123 us
  Pallas kernels  116 us (94%)
  local copies, waits for them, and re-layouts  5.73 us (5%)
  other arithmetic  1.36 us (1%)
    pallas_call x1, Pallas kernels, local(): pl.pallas_call(functools.partial(kernel, n_pipe, tn, td), out_shape=(grad...  116 us
    unnamed x2, local copies, waits for them, and re-layouts  4.32 us

profile of v1, /device:TPU:24, one launch (start us, length us, event | category | flops | bytes accessed | tf_op | source)
XLA Modules:
  0.0 123.4 jit_solution(18167198362229936781)
XLA Ops:
  0.6 1.4 %add_convert_fusion.rt_in = f32[8,128]{1,0:T(8,128)} fusion(s32[2,128]{1,0:T(2,128)} %bitcast.6, s32[2,128]{1,0:T(2,128)} %bitcast.7), kind=kLoop, calls=%fused_computation | loop fusion | flops 4096 | bytes 6144 | tf_op jit(solution)/shard_map/convert_element_type | solution.py:384
  2.0 1.4 %pad.4.rout = bf16[16,3584]{1,0:T(8,128)(2,1)} pad(bf16[4,3584]{1,0:T(4,128)(2,1)} %bitcast.5, bf16[]{:T(256)} %constant.2.clone.1), padding=0_12x0_0 | pad | bytes 143362 | tf_op jit(solution)/shard_map/jit(_pad)/pad | solution.py:385
  3.4 115.7 %relay_slot.1 = (bf16[128,3584]{1,0:T(8,128)(2,1)}, bf16[128,3584]{1,0:T(8,128)(2,1)}) custom-call(bf16[128,3584]{1,0:T(8,128)(2,1)} %sx_hbm.1, bf16[128,3584]{1,0:T(8,128)(2,1)} %z_hbm.1, bf16[128,3584]{1,0:T(8,128)(2,1)} %fx_hbm.1, f32[8,128]{1,0:T(8,128)} %add_convert_fusion.rt_in, f32[1,3584]{1,0:T(1,128)} %gain.1, bf16[16,3584]{1,0:T(8,128)(2,1)} %pad.4.rout, ...), custom_call_target="tpu_custom_call" | custom-call | tf_op jit(solution)/shard_map/relay_slot/pallas_call | solution.py:391
  119.1 2.2 %copy.14 = bf16[128,3584]{1,0:T(8,128)(2,1)} copy(bf16[128,3584]{1,0:T(8,128)(2,1)} %get-tuple-element.4) | data formatting | bytes 1835008
  121.3 2.2 %copy.15 = bf16[128,3584]{1,0:T(8,128)(2,1)} copy(bf16[128,3584]{1,0:T(8,128)(2,1)} %get-tuple-element.5) | data formatting | bytes 1835008

commit v2 on v1

--- a/solution.py
+++ b/solution.py
@@ -18,10 +18,10 @@
 
 def kernel(
     n_pipe, tn, td,
-    sx_hbm, z_hbm, fx_hbm, rt_in, gain, rout, wg_hbm, wu_hbm, wd_hbm,
+    sx_hbm, z_hbm, fx_hbm, rt_s, rt_f, gain, rout, wg_hbm, wu_hbm, wd_hbm,
     fo_hbm, go_hbm,
     sx, z, fx, rts, wg, wu, wd, rb, nrm, hh, dg, du, acc, cols, wb, wf, rcb, rcf, lpb, lpf, at, ar,
-    loc_sem, w_sem, c_send, c_recv, l_send, l_recv, t_send, t_recv, pb_send, pb_recv, pf_send, pf_recv,
+    loc_sem, w_sem, c_send, c_recv, l_send, l_recv, r_send, r_recv, t_send, t_recv, pb_send, pb_recv, pf_send, pf_recv,
     go_send, go_recv, fo_send, fo_recv, zero_sem,
 ):
     c = lax.axis_index("pipe")
@@ -71,12 +71,13 @@
         k = 6 + 2 * i + g
         return remote(src.at[block(2 * g + 1)], dst.at[block(g)], c_send.at[k], c_recv.at[k], core)
 
-    def routes_to(s):
-        return remote(rt_in, rts.at[s], t_send.at[s - 1], t_recv.at[s - 1], (core, link, diag)[s - 1])
+    def routes_to(s, kind):
+        k = 3 * kind + s - 1
+        return remote((rt_s, rt_f)[kind], rts.at[kind, s], r_send.at[k], r_recv.at[k], (core, link, diag)[s - 1])
 
     def dots_to(s):
         t = (None, 3, 0, 1)[s]
-        return remote(at.at[t], ar.at[s], t_send.at[2 + s], t_recv.at[2 + s], (core, link, diag)[s - 1])
+        return remote(at.at[t], ar.at[s], t_send.at[s - 1], t_recv.at[s - 1], (core, link, diag)[s - 1])
 
     def part(q):
         return pl.ds(pl.multiple_of(q * CHUNK, CHUNK), CHUNK)
@@ -110,14 +111,17 @@
     pl.semaphore_wait(barrier, 5)
 
     for s in (1, 2, 3):
-        routes_to(s).start()
+        routes_to(s, 0).start()
+        routes_to(s, 1).start()
     for i in range(3):
         own_to_link(i).start()
         own_to_core(i).start()
 
-    rts[0] = rt_in[...]
+    rts[0, 0] = rt_s[...]
+    rts[1, 0] = rt_f[...]
     rb[...] = jnp.zeros_like(rb)
-    rb[0:16, :] = rout[...]
+    table = rout[...].astype(F32)
+    rb[0:16, :] = jnp.concatenate([table, jnp.zeros((12, width), F32)], axis=0).astype(BF16)
     eye = lax.broadcasted_iota(jnp.int32, (rows, rows), 0) == lax.broadcasted_iota(jnp.int32, (rows, rows), 1)
 
     def to_col(row):
@@ -145,9 +149,8 @@
         out = []
         for h in range(2):
             s = 2 * g + h
-            tile = rts[s]
-            first = 2 - 2 * kind
-            r0, r1 = to_col(tile[first : first + 1, :]), to_col(tile[first + 1 : first + 2, :])
+            tile = rts[kind, s].astype(F32)
+            r0, r1 = to_col(tile[0:1, :]), to_col(tile[1:2, :])
             mine = scores[h * rows : (h + 1) * rows, :]
             q0 = jnp.sum(jnp.where(lane == r0, mine, 0.0), axis=1, keepdims=True)
             q1 = jnp.sum(jnp.where(lane == r1, mine, 0.0), axis=1, keepdims=True)
@@ -239,7 +242,8 @@
     own_to_core(0).wait_recv()
     own_to_core(1).wait_recv()
     for s in (1, 2, 3):
-        routes_to(s).wait_recv()
+        routes_to(s, 0).wait_recv()
+        routes_to(s, 1).wait_recv()
     backward(0, True)
     sums_to_core(0, 0).start()
     dots_to(2).start()
@@ -264,8 +268,8 @@
     pass_to_core(2).start()
     for s in (1, 2, 3):
         dots_to(s).wait_recv()
-    tile = rts[2]
-    r0, r1 = to_col(tile[2:3, :]), to_col(tile[3:4, :])
+    tile = rts[0, 2].astype(F32)
+    r0, r1 = to_col(tile[0:1, :]), to_col(tile[1:2, :])
     saved = cols[...]
     q0, q1 = saved[:, 0:1], saved[:, 1:2]
     total = q0 + q1
@@ -341,7 +345,8 @@
     lax.fori_loop(0, n_chunks, finish_forward, 0)
 
     for s in (1, 2, 3):
-        routes_to(s).wait_send()
+        routes_to(s, 0).wait_send()
+        routes_to(s, 1).wait_send()
         dots_to(s).wait_send()
     for i in range(3):
         own_to_core(i).wait_send()
@@ -374,6 +379,26 @@
         pltpu.make_async_copy(nrm.at[0:rows], go_hbm, zero_sem.at[1]).wait()
 
 
+def settle(f_in, g_in, f_out, g_out, held, in_sem, out_sem):
+    rows = f_in.shape[0]
+    size = rows // 2
+    moves = []
+    for i, (src, dst) in enumerate(((f_in, f_out), (g_in, g_out))):
+        for k in range(2):
+            cut = pl.ds(k * size, size)
+            moves.append((
+                pltpu.make_async_copy(src.at[cut], held.at[i, cut], in_sem.at[i, k]),
+                pltpu.make_async_copy(held.at[i, cut], dst.at[cut], out_sem.at[i, k]),
+            ))
+    for load, _ in moves:
+        load.start()
+    for load, store in moves:
+        load.wait()
+        store.start()
+    for _, store in moves:
+        store.wait()
+
+
 def local(
     n_pipe, fwd_in, fwd_routes, saved_in, saved_routes, grad_in, norm_gain, router, w_gate, w_up, w_down
 ):
@@ -381,8 +406,6 @@
     hidden = w_gate.shape[3]
     tn = min(256, hidden)
     td = 512 if width % 512 == 0 else 128
-    routes = jnp.concatenate([fwd_routes.T, saved_routes.T, fwd_routes.T, saved_routes.T], axis=0).astype(F32)
-    rout = jnp.pad(router[0].T, ((0, 12), (0, 0)))
     n_chunks = rows // CHUNK
     dma = pltpu.SemaphoreType.DMA
     vmem = pl.BlockSpec(memory_space=pltpu.VMEM)
@@ -391,13 +414,13 @@
     fwd_out, grad_out = pl.pallas_call(
         functools.partial(kernel, n_pipe, tn, td),
         out_shape=(grad_out_type, grad_out_type),
-        in_specs=[hbm, hbm, hbm, vmem, vmem, vmem, hbm, hbm, hbm],
+        in_specs=[hbm, hbm, hbm, vmem, vmem, vmem, vmem, hbm, hbm, hbm],
         out_specs=(hbm, hbm),
         scratch_shapes=[
             pltpu.VMEM((4 * rows, width), BF16),
             pltpu.VMEM((4 * rows, width), BF16),
             pltpu.VMEM((4 * rows, width), BF16),
-            pltpu.VMEM((4, 8, rows), F32),
+            pltpu.VMEM((2, 4, 2, rows), jnp.int32),
             pltpu.VMEM((width, hidden), BF16),
             pltpu.VMEM((width, hidden), BF16),
             pltpu.VMEM((hidden, width), BF16),
@@ -420,6 +443,7 @@
             dma((10,)), dma((10,)),
             dma((3,)), dma((3,)),
             dma((6,)), dma((6,)),
+            dma((3,)), dma((3,)),
             dma((n_chunks,)), dma((n_chunks,)),
             dma((n_chunks,)), dma((n_chunks,)),
             dma((n_chunks,)), dma((n_chunks,)),
@@ -430,8 +454,15 @@
             collective_id=0, has_side_effects=True, vmem_limit_bytes=67043328
         ),
         name="relay_slot",
-    )(saved_in, grad_in, fwd_in, routes, norm_gain, rout, w_gate, w_up, w_down)
-    return fwd_out, grad_out
+    )(saved_in, grad_in, fwd_in, saved_routes.T, fwd_routes.T, norm_gain, router[0].T, w_gate, w_up, w_down)
+    return pl.pallas_call(
+        settle,
+        out_shape=(grad_out_type, grad_out_type),
+        in_specs=[hbm, hbm],
+        out_specs=(hbm, hbm),
+        scratch_shapes=[pltpu.VMEM((2, rows, width), BF16), dma((2, 2)), dma((2, 2))],
+        name="settle",
+    )(fwd_out, grad_out)
 
 
 def solution(mesh):

time: 124 us -> 119 us (0.960)
  local copies, waits for them, and re-layouts: 5.73 us -> 0 us
  Pallas kernels: 116 us -> 118 us
  other arithmetic: 1.36 us -> 0 us
    unnamed x2 -> x0, local copies, waits for them, and re-layouts: 4.32 us -> none
    pallas_call x0 -> x1, Pallas kernels: none -> 2.31 us  [local(): pl.pallas_call(settle, out_shape=(grad_out_type, grad_out_type), in_specs...]
    pad x1 -> x0, local copies, waits for them, and re-layouts: 1.41 us -> none  [local(): rout = jnp.pad(router[0].T, ((0, 12), (0, 0)))]
    convert_element_type x1 -> x0, other arithmetic: 1.36 us -> none  [local(): jnp.concatenate([fwd_routes.T, saved_routes.T, fwd_routes.T, saved_routes...]
where the time goes in v2:
time: 119 us
  Pallas kernels  118 us (99%)
    pallas_call x1, Pallas kernels, local(): pl.pallas_call(functools.partial(kernel, n_pipe, tn, td), out_shape=(grad...  116 us

profile of v2, /device:TPU:24, one launch (start us, length us, event | category | flops | bytes accessed | tf_op | source)
XLA Modules:
  0.0 118.6 jit_solution(13009756208546611654)
XLA Ops:
  0.6 115.7 %relay_slot.1 = (bf16[128,3584]{1,0:T(8,128)(2,1)}, bf16[128,3584]{1,0:T(8,128)(2,1)}) custom-call(bf16[128,3584]{1,0:T(8,128)(2,1)} %sx_hbm.1, bf16[128,3584]{1,0:T(8,128)(2,1)} %z_hbm.1, bf16[128,3584]{1,0:T(8,128)(2,1)} %fx_hbm.1, s32[2,128]{1,0:T(2,128)} %bitcast.6, s32[2,128]{1,0:T(2,128)} %bitcast.7, f32[1,3584]{1,0:T(1,128)} %gain.1, ...), custom_call_target="tpu_custom_call" | custom-call | tf_op jit(solution)/shard_map/relay_slot/pallas_call | solution.py:414
  116.3 2.3 %settle.1 = (bf16[128,3584]{1,0:T(8,128)(2,1)}, bf16[128,3584]{1,0:T(8,128)(2,1)}) custom-call(bf16[128,3584]{1,0:T(8,128)(2,1)} %get-tuple-element.4.f_in, bf16[128,3584]{1,0:T(8,128)(2,1)} %get-tuple-element.5.g_in), custom_call_target="tpu_custom_call" | custom-call | tf_op jit(solution)/shard_map/settle/pallas_call | solution.py:458

commit v3 on v2

--- a/solution.py
+++ b/solution.py
@@ -13,6 +13,7 @@
 BF16 = jnp.bfloat16
 NT = (((1,), (1,)), ((), ()))
 CHUNK = 16
+FINE = 16
 STEP = 16
 
 
@@ -79,20 +80,23 @@
         t = (None, 3, 0, 1)[s]
         return remote(at.at[t], ar.at[s], t_send.at[s - 1], t_recv.at[s - 1], (core, link, diag)[s - 1])
 
-    def part(q):
-        return pl.ds(pl.multiple_of(q * CHUNK, CHUNK), CHUNK)
-
-    def tail(q):
-        return pl.ds(pl.multiple_of(2 * rows + q * CHUNK, CHUNK), CHUNK)
+    sizes = (CHUNK, FINE)
+    counts = (rows // CHUNK, rows // FINE)
+
+    def part(i, q):
+        return pl.ds(pl.multiple_of(q * sizes[i], sizes[i]), sizes[i])
+
+    def tail(i, q):
+        return pl.ds(pl.multiple_of(2 * rows + q * sizes[i], sizes[i]), sizes[i])
 
     def sums_to_link(i, q):
         src, dst, send, recv = ((wb, lpb, pb_send, pb_recv), (wf, lpf, pf_send, pf_recv))[i]
-        return remote(src.at[part(q)], dst.at[part(q)], send.at[q], recv.at[q], link)
+        return remote(src.at[part(i, q)], dst.at[part(i, q)], send.at[q], recv.at[q], link)
 
     def result(i, q):
         if i == 0:
-            return remote(wb.at[tail(q)], go_hbm.at[part(q)], go_send.at[q], go_recv.at[q], before)
-        return remote(wf.at[tail(q)], fo_hbm.at[part(q)], fo_send.at[q], fo_recv.at[q], after)
+            return remote(wb.at[tail(0, q)], go_hbm.at[part(0, q)], go_send.at[q], go_recv.at[q], before)
+        return remote(wf.at[tail(1, q)], fo_hbm.at[part(1, q)], fo_send.at[q], fo_recv.at[q], after)
 
     tiles = hidden // tn
     load_x(0).start()
@@ -231,11 +235,12 @@
         sums_to_core(i, 0).wait_recv()
 
         def step(q, _):
-            keep[part(q), :] = (keep[part(q), :].astype(F32) + got[part(q), :].astype(F32)).astype(BF16)
+            cut = part(i, q)
+            keep[cut, :] = (keep[cut, :].astype(F32) + got[cut, :].astype(F32)).astype(BF16)
             sums_to_link(i, q).start()
             return 0
 
-        lax.fori_loop(0, n_chunks, step, 0)
+        lax.fori_loop(0, counts[i], step, 0)
 
     load_x(0).wait()
     load_x(1).wait()
@@ -329,12 +334,10 @@
 
     def finish_forward(q, _):
         sums_to_link(1, q).wait_recv()
-        for k in range(CHUNK // STEP):
-            at_rows = pl.ds(pl.multiple_of(q * CHUNK + k * STEP, STEP), STEP)
-            far = pl.ds(pl.multiple_of(2 * rows + q * CHUNK + k * STEP, STEP), STEP)
-            near = pl.ds(pl.multiple_of(rows + q * CHUNK + k * STEP, STEP), STEP)
-            out = wf[far, :].astype(F32) + rcf[near, :].astype(F32) + lpf[at_rows, :].astype(F32)
-            wf[far, :] = (fx[far, :].astype(F32) + out).astype(BF16)
+        far = tail(1, q)
+        near = pl.ds(pl.multiple_of(rows + q * FINE, FINE), FINE)
+        out = wf[far, :].astype(F32) + rcf[near, :].astype(F32) + lpf[part(1, q), :].astype(F32)
+        wf[far, :] = (fx[far, :].astype(F32) + out).astype(BF16)
 
         @pl.when(c < n_pipe - 1)
         def _():
@@ -342,7 +345,7 @@
 
         return 0
 
-    lax.fori_loop(0, n_chunks, finish_forward, 0)
+    lax.fori_loop(0, counts[1], finish_forward, 0)
 
     for s in (1, 2, 3):
         routes_to(s, 0).wait_send()
@@ -355,19 +358,21 @@
     for i in range(2):
         for g in range(2):
             sums_to_core(i, g).wait_send()
-        for q in range(n_chunks):
+        for q in range(counts[i]):
             sums_to_link(i, q).wait_send()
 
     @pl.when(c > 0)
     def _():
-        for q in range(n_chunks):
+        for q in range(counts[0]):
             result(0, q).wait_send()
+        for q in range(counts[1]):
             result(1, q).wait_recv()
 
     @pl.when(c < n_pipe - 1)
     def _():
-        for q in range(n_chunks):
+        for q in range(counts[1]):
             result(1, q).wait_send()
+        for q in range(counts[0]):
             result(0, q).wait_recv()
 
     @pl.when(c == 0)
@@ -377,26 +382,6 @@
     @pl.when(c == n_pipe - 1)
     def _():
         pltpu.make_async_copy(nrm.at[0:rows], go_hbm, zero_sem.at[1]).wait()
-
-
-def settle(f_in, g_in, f_out, g_out, held, in_sem, out_sem):
-    rows = f_in.shape[0]
-    size = rows // 2
-    moves = []
-    for i, (src, dst) in enumerate(((f_in, f_out), (g_in, g_out))):
-        for k in range(2):
-            cut = pl.ds(k * size, size)
-            moves.append((
-                pltpu.make_async_copy(src.at[cut], held.at[i, cut], in_sem.at[i, k]),
-                pltpu.make_async_copy(held.at[i, cut], dst.at[cut], out_sem.at[i, k]),
-            ))
-    for load, _ in moves:
-        load.start()
-    for load, store in moves:
-        load.wait()
-        store.start()
-    for _, store in moves:
-        store.wait()
 
 
 def local(
@@ -411,11 +396,12 @@
     vmem = pl.BlockSpec(memory_space=pltpu.VMEM)
     hbm = pl.BlockSpec(memory_space=pl.ANY)
     grad_out_type = jax.ShapeDtypeStruct((rows, width), BF16)
+    held_type = pltpu.VMEM((rows, width), BF16)
     fwd_out, grad_out = pl.pallas_call(
         functools.partial(kernel, n_pipe, tn, td),
-        out_shape=(grad_out_type, grad_out_type),
+        out_shape=(held_type, held_type),
         in_specs=[hbm, hbm, hbm, vmem, vmem, vmem, vmem, hbm, hbm, hbm],
-        out_specs=(hbm, hbm),
+        out_specs=(vmem, vmem),
         scratch_shapes=[
             pltpu.VMEM((4 * rows, width), BF16),
             pltpu.VMEM((4 * rows, width), BF16),
@@ -445,24 +431,17 @@
             dma((6,)), dma((6,)),
             dma((3,)), dma((3,)),
             dma((n_chunks,)), dma((n_chunks,)),
+            dma((rows // FINE,)), dma((rows // FINE,)),
             dma((n_chunks,)), dma((n_chunks,)),
-            dma((n_chunks,)), dma((n_chunks,)),
-            dma((n_chunks,)), dma((n_chunks,)),
+            dma((rows // FINE,)), dma((rows // FINE,)),
             dma((2,)),
         ],
         compiler_params=pltpu.CompilerParams(
-            collective_id=0, has_side_effects=True, vmem_limit_bytes=67043328
+            collective_id=0, has_side_effects=True, vmem_limit_bytes=60 * 1024 * 1024
         ),
         name="relay_slot",
     )(saved_in, grad_in, fwd_in, saved_routes.T, fwd_routes.T, norm_gain, router[0].T, w_gate, w_up, w_down)
-    return pl.pallas_call(
-        settle,
-        out_shape=(grad_out_type, grad_out_type),
-        in_specs=[hbm, hbm],
-        out_specs=(hbm, hbm),
-        scratch_shapes=[pltpu.VMEM((2, rows, width), BF16), dma((2, 2)), dma((2, 2))],
-        name="settle",
-    )(fwd_out, grad_out)
+    return fwd_out, grad_out
 
 
 def solution(mesh):

time: 119 us -> 118 us (level)
  Pallas kernels: 118 us -> 116 us
  local copies, waits for them, and re-layouts: 0 us -> 1.85 us
    pallas_call x2 -> x1, Pallas kernels: 118 us -> 116 us  [local(): pl.pallas_call(functools.partial(kernel, n_pipe, tn, td), out_shape=(held...]
    unnamed x0 -> x2, local copies, waits for them, and re-layouts: none -> 1.85 us
where the time goes in v3:
time: 118 us
  Pallas kernels  116 us (98%)
  local copies, waits for them, and re-layouts  1.85 us (2%)
    pallas_call x1, Pallas kernels, local(): pl.pallas_call(functools.partial(kernel, n_pipe, tn, td), out_shape=(held...  116 us

profile of v3, /device:TPU:24, one launch (start us, length us, event | category | flops | bytes accessed | tf_op | source)
XLA Modules:
  0.0 118.1 jit_solution(11607639864183884627)
XLA Ops:
  0.6 115.6 %relay_slot.1 = (bf16[128,3584]{1,0:T(8,128)(2,1)S(1)}, bf16[128,3584]{1,0:T(8,128)(2,1)S(1)}) custom-call(bf16[128,3584]{1,0:T(8,128)(2,1)} %sx_hbm.1, bf16[128,3584]{1,0:T(8,128)(2,1)} %z_hbm.1, bf16[128,3584]{1,0:T(8,128)(2,1)} %fx_hbm.1, s32[2,128]{1,0:T(2,128)} %bitcast.6, s32[2,128]{1,0:T(2,128)} %bitcast.7, f32[1,3584]{1,0:T(1,128)} %gain.1, ...), custom_call_target="tpu_custom_call" | custom-call | tf_op jit(solution)/shard_map/relay_slot/pallas_call | solution.py:400
  116.2 0.9 copy.14
  117.1 0.9 copy.15

commit v4 on v3

--- a/solution.py
+++ b/solution.py
@@ -99,6 +99,10 @@
         return remote(wf.at[tail(1, q)], fo_hbm.at[part(1, q)], fo_send.at[q], fo_recv.at[q], after)
 
     tiles = hidden // tn
+    barrier = pltpu.get_barrier_semaphore()
+    ring = [(lax.rem(c + by, n_pipe), e_l) for by in (1, n_pipe - 1)]
+    for peer in (core, link, diag, *ring):
+        pl.semaphore_signal(barrier, inc=1, device_id=peer, device_id_type=MESH)
     load_x(0).start()
     for j in range(tiles):
         load_w(0, j).start()
@@ -107,11 +111,6 @@
             load_x(1).start()
         load_w(2, j).start()
     load_x(2).start()
-
-    barrier = pltpu.get_barrier_semaphore()
-    ring = [(lax.rem(c + by, n_pipe), e_l) for by in (1, n_pipe - 1)]
-    for peer in (core, link, diag, *ring):
-        pl.semaphore_signal(barrier, inc=1, device_id=peer, device_id_type=MESH)
     pl.semaphore_wait(barrier, 5)
 
     for s in (1, 2, 3):

time: 118 us -> 118 us (level)
  no operation moved by 1% of the time
where the time goes in v4:
time: 118 us
  Pallas kernels  116 us (98%)
  local copies, waits for them, and re-layouts  1.85 us (2%)
    pallas_call x1, Pallas kernels, local(): pl.pallas_call(functools.partial(kernel, n_pipe, tn, td), out_shape=(held...  116 us

profile of v4, /device:TPU:24, one launch (start us, length us, event | category | flops | bytes accessed | tf_op | source)
XLA Modules:
  0.0 118.0 jit_solution(16398592880491047285)
XLA Ops:
  0.6 115.6 %relay_slot.1 = (bf16[128,3584]{1,0:T(8,128)(2,1)S(1)}, bf16[128,3584]{1,0:T(8,128)(2,1)S(1)}) custom-call(bf16[128,3584]{1,0:T(8,128)(2,1)} %sx_hbm.1, bf16[128,3584]{1,0:T(8,128)(2,1)} %z_hbm.1, bf16[128,3584]{1,0:T(8,128)(2,1)} %fx_hbm.1, s32[2,128]{1,0:T(2,128)} %bitcast.6, s32[2,128]{1,0:T(2,128)} %bitcast.7, f32[1,3584]{1,0:T(1,128)} %gain.1, ...), custom_call_target="tpu_custom_call" | custom-call | tf_op jit(solution)/shard_map/relay_slot/pallas_call | solution.py:399
  116.2 0.9 copy.14
  117.1 0.9 copy.15
